TPU v7x, 256 devices: a whole 4x4x8 slice. The times are simulated.
256 devices in a mesh: tm: 16 (over x, y), space: 16 (over z, core).
Axes of the slice: x: 4, y: 4, z: 8, core: 2. Of those that a mesh axis runs over, the one named last changes fastest.
Arguments:
- fields: bfloat16 [16384, 2, 32768], P('tm', None, 'space')
- calendar_day: int32 [16384], P('tm'), may hold values from 0 to 364, as said below
- events: int32 [16, 96], replicated, may hold values from 0 to 16368, as said below
- lag_offsets: int32 [16], replicated, may hold values from 0 to 15, each once
Outputs:
- composite: float32 [16, 16, 2, 32768], P('tm', None, None, 'space')
Inputs may be any that keep to these rules, and one draw needn't show every extreme that they name: `calendar_day`: days of the year of successive record days, one or two calendar days apart. `events`: each entry is a record day; a day may repeat within a type. `lag_offsets`: each of 0 to 15 once.
All inputs are finite; a program needn't handle non-finite values.
Results may differ from a plain program's by a relative error of at most 0.0012.
Values may be sent and summed in bfloat16 or wider, within the bound.
No kernel may reach another device: no remote copies, remote signals or barrier semaphores. Data moves between devices by JAX's collectives and lax.ppermute only.
A program may use at most 64 MiB of HBM per device.

v0:
```python
import jax
import jax.numpy as jnp
from jax import lax
from jax.sharding import PartitionSpec as P

HARMONICS = 4


TWO_PI = 6.283185307179586


def from_everyone(value, axis):
    copies = jnp.broadcast_to(value, (lax.axis_size(axis), *value.shape))
    return lax.all_to_all(copies, axis, split_axis=0, concat_axis=0, tiled=True)


def of_everyone(value, axis):
    everything = from_everyone(value, axis)
    return jnp.sum(everything, axis=0)


def in_one(arrays, axis):
    ends = [0]
    for a in arrays:
        ends.append(ends[-1] + a.size)
    total = of_everyone(jnp.concatenate([a.ravel() for a in arrays]), axis)
    return tuple((total[b:e].reshape(a.shape) for a, b, e in zip(arrays, ends, ends[1:])))


def in_blocks(value, dim, peers):
    shape = value.shape
    parts = value.reshape(*shape[:dim], peers, shape[dim] // peers, *shape[dim + 1 :])
    return jnp.moveaxis(parts, dim, 0)


def sent_and_summed(value, axis, dim):
    parts = in_blocks(value, dim, lax.axis_size(axis))
    arrived = lax.all_to_all(parts, axis, split_axis=0, concat_axis=0, tiled=True)
    return arrived.sum(axis=0)


def regressors(calendar_day):
    phases = calendar_day.astype(jnp.float32) * (TWO_PI / 365.25)
    columns = [jnp.ones_like(phases)]
    for harmonic in range(1, HARMONICS + 1):
        columns.append(jnp.cos(harmonic * phases))
        columns.append(jnp.sin(harmonic * phases))
    return jnp.stack(columns, axis=1).astype(jnp.bfloat16)


def solve_fit(gram_matrix, projection):
    factor = jnp.linalg.cholesky(gram_matrix)
    return jax.scipy.linalg.cho_solve((factor, True), projection)


def fit_coefficients(gram_matrix, projection):
    gram_matrix, projection = in_one((gram_matrix, projection), "tm")
    return solve_fit(gram_matrix, projection)


def day_counts(events, lag_offsets, first_day, length):
    lag_count = lag_offsets.shape[0]
    day_numbers = first_day - (lag_count - 1) + lax.iota(jnp.int32, length + lag_count - 1)

    def type_histogram(event_row):
        matches = event_row[:, None] == day_numbers[None, :]
        return jnp.sum(matches.astype(jnp.float32), axis=0)

    histogram = lax.map(type_histogram, events).astype(jnp.bfloat16)
    shifted = jnp.stack(
        [
            lax.slice_in_dim(
                histogram, lag_count - 1 - offset, lag_count - 1 - offset + length, axis=1
            )
            for offset in range(lag_count)
        ]
    )
    lag_select = (lag_offsets[:, None] == lax.iota(jnp.int32, lag_count)[None, :]).astype(
        jnp.bfloat16
    )
    counts = jnp.einsum("ls,set->elt", lag_select, shifted, preferred_element_type=jnp.float32)
    return counts.astype(jnp.bfloat16).reshape(-1, length)


def shards(fields, calendar_day, events, lag_offsets):
    members = events.shape[1]
    lag_count = lag_offsets.shape[0]
    local_days = fields.shape[0]
    local_points = fields.shape[2]
    record = fields.reshape(local_days, 2 * local_points)
    design = regressors(calendar_day)
    gram_matrix = jnp.dot(design.T, design, preferred_element_type=jnp.float32)
    projection = jnp.dot(design.T, record, preferred_element_type=jnp.float32)
    counts = day_counts(events, lag_offsets, lax.axis_index("tm") * local_days, local_days)
    counted_design = jnp.dot(counts, design, preferred_element_type=jnp.float32)
    coefficients = fit_coefficients(gram_matrix, projection)
    raw_part = jnp.dot(counts, record, preferred_element_type=jnp.float32)
    totals = sent_and_summed(
        raw_part - jnp.dot(counted_design, coefficients, precision=lax.Precision.HIGHEST), "tm", 0
    )
    maps = (totals / members).reshape(-1, lag_count, 2, local_points)
    map_sums = of_everyone(jnp.sum(maps, axis=3, keepdims=True), "space")
    return maps - map_sums / (local_points * lax.axis_size("space"))


def solution(mesh):
    return jax.shard_map(
        shards,
        mesh=mesh,
        in_specs=(P("tm", None, "space"), P("tm"), P(), P()),
        out_specs=P("tm", None, None, "space"),
        check_vma=False,
    )
```

profile of v0, /device:TPU:1, one launch (start us, length us, event | category | flops | bytes accessed | tf_op | source)
XLA Modules:
  0.0 147.8 jit_solution(3158510713344325320)
XLA Ops:
  0.0 12.0 %copy.377 = bf16[128,8,2,2048]{3,1,2,0:T(8,128)(2,1)} copy(bf16[128,8,2,2048]{3,2,1,0:T(2,128)(2,1)} %bitcast.74) | data formatting | bytes 16777216
  12.4 4.6 %fusion.14 = f32[9,4096]{1,0:T(8,128)S(1)} fusion(bf16[1024,9]{0,1:T(8,128)(2,1)S(1)} %stack.112, bf16[1024,4096]{1,0:T(8,128)(2,1)} %bitcast.71), kind=kOutput, calls=%fused_computation.56 | convolution fusion | flops 75497472 | bytes 8554496 | tf_op jit(solution)/shard_map/dot_general | solution.py:93
  17.2 2.7 %broadcast_in_dim.21 = f32[16,1,36945]{2,1,0:T(1,128)} broadcast(f32[36945]{0:T(1024)S(1)} %pad_maximum_fusion), dimensions={2} | broadcast | bytes 2512260 | tf_op jit(solution)/shard_map/broadcast_in_dim | solution.py:13
  19.9 7.7 %all-to-all-start = ((f32[16,1,36945]{2,1,0:T(1,128)}), f32[16,1,36945]{2,1,0:T(1,128)S(1)}, u32[]{:S(2)}, u32[]{:S(2)}) async-start(f32[16,1,36945]{2,1,0:T(1,128)} %broadcast_in_dim.21), calls=%async_computation | async-start | bytes 4734976 | tf_op jit(solution)/shard_map/all_to_all | solution.py:14
  27.6 15.2 %while.11 = (s32[]{:T(128)}, bf16[16,1039]{1,0:T(8,128)(2,1)S(1)}, s32[16,96]{1,0:T(8,128)}, s32[]{:T(128)}, s32[]{:T(128)}, /*index=5*/s32[]{:T(128)}) while((s32[]{:T(128)}, bf16[16,1039]{1,0:T(8,128)(2,1)S(1)}, s32[16,96]{1,0:T(8,128)}, s32[]{:T(128)}, s32[]{:T(128)}, /*index=5*/s32[]{:T(128)}) %tuple.43), condition=%wide.region_2.3_spmd.clone, body=%wide.region_0.2_spmd.clone.sunk | while | flops 299234 | bytes 19943 | solution.py:69
  27.7 0.7 dynamic-slice_bitcast_fusion.2
  28.6 0.7 dynamic-slice_bitcast_fusion.2
  29.6 0.7 dynamic-slice_bitcast_fusion.2
  30.5 0.7 dynamic-slice_bitcast_fusion.2
  31.5 0.7 dynamic-slice_bitcast_fusion.2
  32.4 0.7 dynamic-slice_bitcast_fusion.2
  33.4 0.7 dynamic-slice_bitcast_fusion.2
  34.3 0.7 dynamic-slice_bitcast_fusion.2
  35.3 0.7 dynamic-slice_bitcast_fusion.2
  36.2 0.7 dynamic-slice_bitcast_fusion.2
  37.2 0.7 dynamic-slice_bitcast_fusion.2
  38.1 0.7 dynamic-slice_bitcast_fusion.2
  39.1 0.7 dynamic-slice_bitcast_fusion.2
  40.1 0.7 dynamic-slice_bitcast_fusion.2
  41.0 0.7 dynamic-slice_bitcast_fusion.2
  42.0 0.7 dynamic-slice_bitcast_fusion.2
  42.9 0.2 slice_bitcast_fusion
  43.6 0.7 copy.362
  44.3 0.7 copy.363
  45.0 0.7 copy.364
  45.7 0.7 copy.365
  46.3 0.7 copy.366
  47.0 0.7 copy.367
  47.7 0.7 copy.368
  48.3 2.4 %stack.103 = bf16[16,16,1024]{2,0,1:T(8,128)(2,1)S(1)} concatenate(bf16[1,16,1024]{2,0,1:T(2,128)(2,1)S(1)} %copy.353, bf16[1,16,1024]{2,0,1:T(2,128)(2,1)S(1)} %copy.354, bf16[1,16,1024]{2,0,1:T(2,128)(2,1)S(1)} %copy.355, bf16[1,16,1024]{2,0,1:T(2,128)(2,1)S(1)} %copy.356, bf16[1,16,1024]{2,0,1:T(2,128)(2,1)S(1)} %copy.357, bf16[1,16,1024]{2,0,1:T(2,128)(2,1)S(1)} %copy.358, ...), dimensions={0} | concatenate | bytes 1048576 | tf_op jit(solution)/shard_map/stack | solution.py:70
  50.8 0.4 convolution_convert_fusion
  51.2 0.2 fusion.12
  51.4 7.7 %fusion.11 = f32[256,4096]{1,0:T(8,128)} fusion(bf16[256,1024]{1,0:T(8,128)(2,1)S(1)} %bitcast.76, bf16[1024,4096]{1,0:T(8,128)(2,1)} %bitcast.72), kind=kOutput, calls=%fused_computation.53 | convolution fusion | flops 2147483648 | bytes 13107200 | tf_op jit(solution)/shard_map/dot_general | solution.py:97
  59.1 0.4 all-to-all-done
  59.5 1.5 %reduce_sum.45 = f32[36945]{0:T(1024)S(1)} reduce(f32[16,1,36945]{2,1,0:T(1,128)S(1)} %all-to-all-done, f32[]{:T(128)} %constant.79.clone.1), dimensions={0,1}, to_apply=%region_3.4 | reduce | flops 554175 | bytes 2512264 | tf_op jit(solution)/shard_map/reduce_sum | solution.py:19
  61.4 0.8 cholesky.16
  62.2 0.6 compare_reduce_fusion
  62.9 0.6 fusion.2
  63.5 0.7 custom-call.10
  64.2 0.4 fusion.3
  64.7 0.3 fusion.5
  65.0 5.4 %convolution_subtract_fusion = f32[256,4096]{1,0:T(8,128)S(1)} fusion(f32[256,4096]{1,0:T(8,128)} %fusion.11, f32[256,9]{0,1:T(8,128)S(1)} %fusion.12, f32[9,4096]{1,0:T(8,128)S(1)} %fusion.5), kind=kOutput, calls=%fused_computation.4 | convolution fusion | flops 114294784 | bytes 8545280 | tf_op jit(solution)/shard_map/dot_general | solution.py:99
  70.4 54.4 %all_to_all.16 = f32[16,16,4096]{2,1,0:T(8,128)} all-to-all(f32[16,16,4096]{2,1,0:T(8,128)S(1)} %bitcast.73), channel_id=1, replica_groups=mesh['tm'=16,'space'=16] {'tm'}, dimensions={0} | all-to-all | bytes 8388608 | tf_op jit(solution)/shard_map/all_to_all | solution.py:38
  124.8 2.4 %reduce_sum.46 = f32[16,4096]{1,0:T(8,128)S(1)} reduce(f32[16,16,4096]{2,1,0:T(8,128)} %all_to_all.16, f32[]{:T(128)} %constant.79.clone.1), dimensions={0}, to_apply=%region_6.7 | reduce | flops 983040 | bytes 4456452 | tf_op jit(solution)/shard_map/reduce_sum | solution.py:39
  127.3 0.2 div.26
  127.5 0.2 reduce_sum.47
  127.8 19.0 %all_to_all.17 = f32[16,1,16,2,1]{2,3,4,1,0:T(2,128)S(1)} all-to-all(f32[16,1,16,2,1]{2,3,4,1,0:T(2,128)S(1)} %broadcast_in_dim.22), channel_id=1, replica_groups=mesh['tm'=16,'space'=16] {'space'}, dimensions={0} | all-to-all | bytes 4096 | tf_op jit(solution)/shard_map/all_to_all | solution.py:14
  146.9 0.9 broadcast_subtract_fusion
  (106 shorter events, 5.2 us)
Async XLA Ops:
  0.0 12.0 %copy-start = (s32[1024]{0:T(1024)S(1)}, s32[1024]{0:T(1024)}, u32[]{:S(2)}) copy-start(s32[1024]{0:T(1024)} %param.7) | copy-start | bytes 12292
  19.9 30.9 %copy-start.1 = (s32[16]{0:T(128)S(1)}, s32[16]{0:T(128)}, u32[]{:S(2)}) copy-start(s32[16]{0:T(128)} %param.9) | copy-start | bytes 196
  19.9 39.6 %all-to-all-start = ((f32[16,1,36945]{2,1,0:T(1,128)}), f32[16,1,36945]{2,1,0:T(1,128)S(1)}, u32[]{:S(2)}, u32[]{:S(2)}) async-start(f32[16,1,36945]{2,1,0:T(1,128)} %broadcast_in_dim.21), calls=%async_computation | async-start | bytes 4734976 | tf_op jit(solution)/shard_map/all_to_all | solution.py:14
where the time goes:
time: 149 us; the launch traced here: 148 us
  blocking collectives  73.5 us (49%)
  local copies, waits for them, and re-layouts  35.9 us (24%)
  matrix products  19.2 us (13%)
  other arithmetic  10.2 us (7%)
  starting transfers between devices  7.71 us (5%)
    all_to_all x1, blocking collectives, sent_and_summed(): lax.all_to_all(parts, axis, split_axis=0, concat_axis=0, tiled=True)  54.4 us
    all_to_all x1, blocking collectives, from_everyone(): return lax.all_to_all(copies, axis, split_axis=0, concat_axis=0, tiled=True)  19 us
    unnamed x5, local copies, waits for them, and re-layouts  12 us
    eq x16, local copies, waits for them, and re-layouts, type_histogram(): matches = event_row[:, None] == day_numbers[None, :]  11.2 us
    another operation x18, local copies, waits for them, and re-layouts, day_counts(): jnp.stack([lax.slice_in_dim(histogram, lag_count - 1 - offset, lag_count...  7.8 us
    dot_general x1, matrix products, shards(): raw_part = jnp.dot(counts, record, preferred_element_type=jnp.float32)  7.72 us
    all_to_all x1, starting transfers between devices, from_everyone(): return lax.all_to_all(copies, axis, split_axis=0, concat_axis=0, tiled=True)  7.71 us
    dot_general x1, matrix products, shards(): jnp.dot(counted_design, coefficients, precision=lax.Precision.HIGHEST)  5.38 us
  transfers between devices with their start and end apart: 1, of which 1 were waited for; matrix products, arithmetic and copies ran while one was open for 21% of the time, Pallas kernels for 0%

commit v1 on v0

v1 whole, which is shorter than its diff:
```python
import jax
import jax.numpy as jnp
from jax import lax
from jax.experimental import pallas as pl
from jax.experimental.pallas import tpu as pltpu
from jax.sharding import PartitionSpec as P

HARMONICS = 4
TWO_PI = 6.283185307179586
TERMS = 2 * HARMONICS + 1
SIDE = 4
TILE = 16
EXTRA = 128
F32 = jnp.float32
BF16 = jnp.bfloat16


def iota(shape, axis):
    return lax.broadcasted_iota(jnp.int32, shape, axis)


def dot(a, b):
    return jnp.dot(a, b, preferred_element_type=F32)


def dot_nt(a, b):
    return lax.dot_general(a, b, (((1,), (1,)), ((), ())), preferred_element_type=F32)


def design_rows(days):
    count = days.shape[1]
    phases = days.astype(F32) * (TWO_PI / 365.25)
    row = iota((TILE, count), 0)
    angles = ((row + 1) // 2).astype(F32) * phases
    waves = jnp.where(row % 2 == 1, jnp.cos(angles), jnp.sin(angles))
    rows = jnp.where(row == 0, 1.0, jnp.where(row < TERMS, waves, 0.0))
    return rows.astype(BF16)


def left_factor(me, events_ref, days_ref, left_ref):
    types, members = events_ref.shape
    lags = TILE
    local_days = days_ref.shape[1]
    rows = types * lags
    window = local_days + 128
    events = events_ref[...] - (me * local_days - 128)
    spot = iota((types, window), 1)
    histogram = jnp.zeros((types, window), F32)
    for m in range(members):
        histogram = histogram + jnp.where(events[:, m : m + 1] == spot, 1.0, 0.0)
    counts = jnp.concatenate(
        [histogram[:, 128 - o : 128 - o + local_days].astype(BF16) for o in range(lags)], axis=0
    )
    design = design_rows(days_ref[...])
    out_row = iota((rows, rows), 0)
    in_row = iota((rows, rows), 1)
    first, second, lag = out_row // (SIDE * lags), out_row // lags % SIDE, out_row % lags
    for v in range(2):
        rank = first * SIDE + second if v == 0 else second * SIDE + first
        order = (in_row == lag * types + (rank ^ me)).astype(F32).astype(BF16)
        spread = (iota((128, 256), 1) == 2 * iota((128, 256), 0) + v).astype(F32).astype(BF16)
        top = v * (rows + TILE)
        ordered = dot(order, counts).astype(BF16)
        for b in range(local_days // 128):
            day = slice(128 * b, 128 * b + 128)
            to = slice(256 * b, 256 * b + 256)
            left_ref[top : top + rows, to] = dot(ordered[:, day], spread).astype(BF16)
            left_ref[top + rows : top + rows + TILE, to] = dot(design[:, day], spread).astype(BF16)


def products_kernel(me_ref, events_ref, days_ref, fields_ref, *refs):
    outs, left_ref = refs[:-1], refs[-1]
    step = pl.program_id(0)
    width = fields_ref.shape[2]
    points = outs[0].shape[1] - EXTRA
    group = outs[0].shape[0] - TILE
    rows = SIDE * group

    def put(value, columns):
        for v in range(2):
            top = v * (rows + TILE)
            for r in range(SIDE):
                out = outs[SIDE * v + r]
                out[:group, columns] = value[top + group * r : top + group * (r + 1)]
                out[group:, columns] = value[top + rows : top + rows + TILE]

    @pl.when(step == 0)
    def _():
        left_factor(me_ref[0], events_ref, days_ref, left_ref)
        halves = []
        for v in range(2):
            left = left_ref[v * (rows + TILE) : (v + 1) * (rows + TILE), :]
            design = left[rows:, :]
            pad = jnp.zeros((EXTRA - TILE, left.shape[1]), BF16)
            halves.append(dot_nt(left, jnp.concatenate([design, pad], axis=0)))
        put(jnp.concatenate(halves, axis=0), slice(points, points + EXTRA))

    record = fields_ref.reshape(2 * fields_ref.shape[0], width)[...]
    put(dot(left_ref[...], record), pl.ds(pl.multiple_of(step * width, width), width))


def products(me, events, days, fields):
    local_days, _, points = fields.shape
    types = events.shape[0]
    group = types * TILE // SIDE
    width = 512
    columns = points + EXTRA
    message = jax.ShapeDtypeStruct((group + TILE, columns), F32)
    whole = pl.BlockSpec((group + TILE, columns), lambda i, me: (0, 0), pipeline_mode=pl.Buffered(1))
    return pl.pallas_call(
        products_kernel,
        grid_spec=pltpu.PrefetchScalarGridSpec(
            num_scalar_prefetch=1,
            grid=(points // width,),
            in_specs=[
                pl.BlockSpec(events.shape, lambda i, me: (0, 0)),
                pl.BlockSpec((1, local_days), lambda i, me: (0, 0)),
                pl.BlockSpec((local_days, 2, width), lambda i, me: (0, 0, i)),
            ],
            out_specs=[whole] * (2 * SIDE),
            scratch_shapes=[pltpu.VMEM((2 * (types * TILE + TILE), 2 * local_days), BF16)],
        ),
        out_shape=[message] * (2 * SIDE),
        name="products",
    )(me, events, days.reshape(1, local_days), fields)


def merge_kernel(*refs):
    taken, outs = refs[:SIDE], refs[SIDE:]
    total = taken[0][...]
    for t in taken[1:]:
        total = total + t[...]
    last = total.shape[0] - TILE
    for r, out in enumerate(outs):
        out[:TILE, :] = total[TILE * r : TILE * (r + 1)]
        out[TILE:, :] = total[last:]


def merge(taken):
    columns = taken[0].shape[1]
    out = jax.ShapeDtypeStruct((2 * TILE, columns), F32)
    return pl.pallas_call(merge_kernel, out_shape=[out] * SIDE, name="merge")(*taken)


def finish_kernel(members, lags_ref, *refs):
    taken, (maps_ref, sums_ref, rows_ref) = refs[: 2 * SIDE], refs[2 * SIDE :]
    lags, _, points = maps_ref.shape
    for v in range(2):
        total = taken[SIDE * v][...]
        for t in taken[SIDE * v + 1 : SIDE * (v + 1)]:
            total = total + t[...]
        row = iota((2 * TILE, 1), 0)
        for k in range(TERMS):
            pivot = total[TILE + k : TILE + k + 1, :]
            column = points + k
            factor = total[:, column : column + 1] / pivot[:, column : column + 1]
            factor = jnp.where((row < TILE) | (row > TILE + k), factor, 0.0)
            total = total - factor * pivot
        rows_ref[...] = total[:TILE, :points] / members
        for l in range(lags):
            line = rows_ref[pl.ds(lags_ref[l], 1), :]
            maps_ref[l, v : v + 1, :] = line
            sums_ref[l, v : v + 1, :] = jnp.broadcast_to(jnp.sum(line, axis=1, keepdims=True), (1, 128))


def finish(members, lag_offsets, taken):
    points = taken[0].shape[1] - EXTRA
    lags = lag_offsets.shape[0]
    return pl.pallas_call(
        lambda *refs: finish_kernel(members, *refs),
        grid_spec=pltpu.PrefetchScalarGridSpec(
            num_scalar_prefetch=1,
            grid=(1,),
            in_specs=[pl.BlockSpec(t.shape, lambda i, lags: (0, 0)) for t in taken],
            out_specs=[
                pl.BlockSpec((lags, 2, points), lambda i, lags: (0, 0, 0)),
                pl.BlockSpec((lags, 2, 128), lambda i, lags: (0, 0, 0)),
            ],
            scratch_shapes=[pltpu.VMEM((TILE, points), F32)],
        ),
        out_shape=[
            jax.ShapeDtypeStruct((lags, 2, points), F32),
            jax.ShapeDtypeStruct((lags, 2, 128), F32),
        ],
        name="finish",
    )(lag_offsets, *taken)


def swap(value, axis, mask):
    return lax.ppermute(value, axis, [(i, i ^ mask) for i in range(lax.axis_size(axis))])


def shards(fields, calendar_day, events, lag_offsets):
    me = lax.axis_index("tm").astype(jnp.int32).reshape(1)
    points = fields.shape[2]
    sent = products(me, events, calendar_day, fields)
    mine = [[sent[0]] + [None] * 3, [sent[SIDE]] + [None] * 3]
    for r in (2, 1, 3):
        mine[0][r] = swap(sent[r], "tm", SIDE * r)
        mine[1][r] = swap(sent[SIDE + r], "tm", r)
    taken = []
    for v in range(2):
        parts = merge(mine[v])
        taken += [parts[0]] + [swap(parts[r], "tm", r if v == 0 else SIDE * r) for r in (1, 2, 3)]
    maps, sums = finish(events.shape[1], lag_offsets, taken)
    for mask in (1, 2, 6, 14):
        sums = sums + swap(sums, "space", mask)
    mean = sums[:, :, :1] / (points * lax.axis_size("space"))
    return (maps - mean)[None]


def solution(mesh):
    return jax.shard_map(
        shards,
        mesh=mesh,
        in_specs=(P("tm", None, "space"), P("tm"), P(), P()),
        out_specs=P("tm", None, None, "space"),
        check_vma=False,
    )
```

time: 149 us -> 116 us (0.78)
  blocking collectives: 73.5 us -> 0 us
  waiting for transfers between devices: 0.44 us -> 45.1 us
  starting transfers between devices: 7.71 us -> 42.7 us
  local copies, waits for them, and re-layouts: 35.9 us -> 1.75 us
  Pallas kernels: 0 us -> 21.9 us
  matrix products: 19.2 us -> 0 us
  other arithmetic: 10.2 us -> 2.57 us
    all_to_all x2 -> x0, blocking collectives: 73.5 us -> none  [the longest x1 54.4 us: sent_and_summed(): lax.all_to_all(parts, axis, split_axis=0, concat_axis=0, tiled=True)]
    ppermute x0 -> x16, waiting for transfers between devices: none -> 45.1 us  [swap(): lax.ppermute(value, axis, [(i, i ^ mask) for i in range(lax.axis_size(axi...]
    ppermute x0 -> x16, starting transfers between devices: none -> 42.7 us  [swap(): lax.ppermute(value, axis, [(i, i ^ mask) for i in range(lax.axis_size(axi...]
    pallas_call x0 -> x4, Pallas kernels: none -> 21.9 us  [the longest x1 12.2 us: products(): pl.pallas_call(products_kernel, grid_spec=pltpu.PrefetchScalarGridSpec(nu...]
    dot_general x6 -> x0, matrix products: 18.4 us -> none  [the longest x1 7.72 us: shards(): raw_part = jnp.dot(counts, record, preferred_element_type=jnp.float32)]
    eq x16 -> x0, local copies, waits for them, and re-layouts: 11.2 us -> none  [type_histogram(): matches = event_row[:, None] == day_numbers[None, :]]
    unnamed x5 -> x22, local copies, waits for them, and re-layouts: 12 us -> 1.58 us
    another operation x28 -> x0, local copies, waits for them, and re-layouts: 7.93 us -> none  [the longest x18 7.8 us: day_counts(): jnp.stack([lax.slice_in_dim(histogram, lag_count - 1 - offset, lag_count...]
  transfers between devices with their start and end apart: 1 -> 16, of which waited for: 1 -> 11; matrix products, arithmetic and copies ran while one was open for 21% -> 0% of each run, Pallas kernels for 0% -> 5%
where the time goes in v1:
time: 116 us; the launch traced here: 114 us
  waiting for transfers between devices  45.1 us (39%)
  starting transfers between devices  42.7 us (37%)
  Pallas kernels  21.9 us (19%)
  other arithmetic  2.57 us (2%)
  local copies, waits for them, and re-layouts  1.75 us (2%)
    ppermute x16, waiting for transfers between devices, swap(): lax.ppermute(value, axis, [(i, i ^ mask) for i in range(lax.axis_size(axi...  45.1 us
    ppermute x16, starting transfers between devices, swap(): lax.ppermute(value, axis, [(i, i ^ mask) for i in range(lax.axis_size(axi...  42.7 us
    pallas_call x1, Pallas kernels, products(): pl.pallas_call(products_kernel, grid_spec=pltpu.PrefetchScalarGridSpec(nu...  12.2 us
    pallas_call x2, Pallas kernels, merge(): pl.pallas_call(merge_kernel, out_shape=[out] * SIDE, name='merge')(*taken)  5.6 us
    pallas_call x1, Pallas kernels, finish(): pl.pallas_call(lambda *refs: finish_kernel(members, *refs), grid_spec=plt...  4.01 us
  transfers between devices with their start and end apart: 16, of which 11 were waited for; matrix products, arithmetic and copies ran while one was open for 0% of the time, Pallas kernels for 5%

profile of v1, /device:TPU:1, one launch (start us, length us, event | category | flops | bytes accessed | tf_op | source)
XLA Modules:
  0.0 114.1 jit_solution(12802693979818626269)
XLA Ops:
  0.0 12.2 %products.1 = (f32[80,2176]{1,0:T(8,128)}, f32[80,2176]{1,0:T(8,128)}, f32[80,2176]{1,0:T(8,128)}, f32[80,2176]{1,0:T(8,128)}, f32[80,2176]{1,0:T(8,128)}, /*ind...) custom-call(s32[1]{0:T(128)} %bitcast.me_ref, s32[16,96]{1,0:T(8,128)} %events_ref.1, s32[1,1024]{1,0:T(1,128)} %bitcast.5, ...), custom_call_target="tpu_custom_call" | custom-call | tf_op jit(solution)/shard_map/products/pallas_call | solution.py:110
  12.3 2.0 %collective-permute-start = (f32[80,2176]{1,0:T(8,128)}, f32[80,2176]{1,0:T(8,128)S(1)}, u32[]{:S(2)}, u32[]{:S(2)}) collective-permute-start(f32[80,2176]{1,0:T(8,128)} %get-tuple-element.24), channel_id=1, source_target_pairs={{0,64},{16,80},{32,96},{48,112},{64,0},{80,16},{96,32},{112,48},{1... | collective-permute-start | bytes 2088968 | tf_op jit(solution)/shard_map/ppermute | solution.py:190
  14.3 2.5 %collective-permute-start.1 = (f32[80,2176]{1,0:T(8,128)}, f32[80,2176]{1,0:T(8,128)S(1)}, u32[]{:S(2)}, u32[]{:S(2)}) collective-permute-start(f32[80,2176]{1,0:T(8,128)} %get-tuple-element.25), channel_id=1, source_target_pairs={{0,128},{16,144},{32,160},{48,176},{64,192},{80,208},{96,224},{112... | collective-permute-start | bytes 2088968 | tf_op jit(solution)/shard_map/ppermute | solution.py:190
  16.7 0.0 collective-permute-start.2
  16.7 1.5 %collective-permute-start.6 = (f32[80,2176]{1,0:T(8,128)}, f32[80,2176]{1,0:T(8,128)S(1)}, u32[]{:S(2)}, u32[]{:S(2)}) collective-permute-start(f32[80,2176]{1,0:T(8,128)} %get-tuple-element.32), channel_id=1, source_target_pairs={{0,16},{16,0},{32,48},{48,32},{64,80},{80,64},{96,112},{112,96},{1... | collective-permute-start | bytes 2088968 | tf_op jit(solution)/shard_map/ppermute | solution.py:190
  18.2 2.6 %collective-permute-start.7 = (f32[80,2176]{1,0:T(8,128)}, f32[80,2176]{1,0:T(8,128)S(1)}, u32[]{:S(2)}, u32[]{:S(2)}) collective-permute-start(f32[80,2176]{1,0:T(8,128)} %get-tuple-element.33), channel_id=1, source_target_pairs={{0,32},{16,48},{32,0},{48,16},{64,96},{80,112},{96,64},{112,80},{1... | collective-permute-start | bytes 2088968 | tf_op jit(solution)/shard_map/ppermute | solution.py:190
  20.8 7.8 %collective-permute-done.refs_1_ = f32[80,2176]{1,0:T(8,128)S(1)} collective-permute-done((f32[80,2176]{1,0:T(8,128)}, f32[80,2176]{1,0:T(8,128)S(1)}, u32[]{:S(2)}, u32[]{:S(2)}) %collective-permute-start) | collective-permute-done | bytes 696352 | tf_op jit(solution)/shard_map/ppermute | solution.py:190
  28.7 4.0 %collective-permute-start.8 = (f32[80,2176]{1,0:T(8,128)}, f32[80,2176]{1,0:T(8,128)S(1)}, u32[]{:S(2)}, u32[]{:S(2)}) collective-permute-start(f32[80,2176]{1,0:T(8,128)} %get-tuple-element.34), channel_id=1, source_target_pairs={{0,48},{16,32},{32,16},{48,0},{64,112},{80,96},{96,80},{112,64},{1... | collective-permute-start | bytes 2088968 | tf_op jit(solution)/shard_map/ppermute | solution.py:190
  32.6 14.3 %collective-permute-done.1.refs_2_ = f32[80,2176]{1,0:T(8,128)S(1)} collective-permute-done((f32[80,2176]{1,0:T(8,128)}, f32[80,2176]{1,0:T(8,128)S(1)}, u32[]{:S(2)}, u32[]{:S(2)}) %collective-permute-start.1) | collective-permute-done | bytes 696352 | tf_op jit(solution)/shard_map/ppermute | solution.py:190
  46.9 2.2 %collective-permute-done.2.refs_3_ = f32[80,2176]{1,0:T(8,128)} collective-permute-done((f32[80,2176]{1,0:T(8,128)}, f32[80,2176]{1,0:T(8,128)}, u32[]{:S(2)}, u32[]{:S(2)}) %collective-permute-start.2) | collective-permute-done | bytes 696352 | tf_op jit(solution)/shard_map/ppermute | solution.py:190
  49.1 0.0 copy-done.3
  49.1 0.0 copy-done.4
  49.1 2.8 %merge.2 = (f32[32,2176]{1,0:T(8,128)}, f32[32,2176]{1,0:T(8,128)}, f32[32,2176]{1,0:T(8,128)}, f32[32,2176]{1,0:T(8,128)}) custom-call(f32[80,2176]{1,0:T(8,128)} %get-tuple-element.23.refs_0_, f32[80,2176]{1,0:T(8,128)} %copy-done.3, f32[80,2176]{1,0:T(8,128)} %copy-done.4, f32[80,2176]{1,0:T(8,128)} %collective-permute-done.2.refs_3_), custom_call_target="tpu_custom_call" | custom-call | tf_op jit(solution)/shard_map/merge/pallas_call | solution.py:142
  51.9 1.3 %collective-permute-start.3 = (f32[32,2176]{1,0:T(8,128)}, f32[32,2176]{1,0:T(8,128)S(1)}, u32[]{:S(2)}, u32[]{:S(2)}) collective-permute-start(f32[32,2176]{1,0:T(8,128)} %get-tuple-element.28), channel_id=1, source_target_pairs={{0,16},{16,0},{32,48},{48,32},{64,80},{80,64},{96,112},{112,96},{1... | collective-permute-start | bytes 835592 | tf_op jit(solution)/shard_map/ppermute | solution.py:190
  53.2 2.6 %collective-permute-start.4 = (f32[32,2176]{1,0:T(8,128)}, f32[32,2176]{1,0:T(8,128)S(1)}, u32[]{:S(2)}, u32[]{:S(2)}) collective-permute-start(f32[32,2176]{1,0:T(8,128)} %get-tuple-element.29), channel_id=1, source_target_pairs={{0,32},{16,48},{32,0},{48,16},{64,96},{80,112},{96,64},{112,80},{1... | collective-permute-start | bytes 835592 | tf_op jit(solution)/shard_map/ppermute | solution.py:190
  55.8 0.0 collective-permute-done.6.refs_1_
  55.8 0.0 collective-permute-start.5
  55.8 0.0 collective-permute-done.7.refs_2_
  55.9 0.0 copy-start.1
  55.9 6.2 %collective-permute-done.8.refs_3_ = f32[80,2176]{1,0:T(8,128)S(1)} collective-permute-done((f32[80,2176]{1,0:T(8,128)}, f32[80,2176]{1,0:T(8,128)S(1)}, u32[]{:S(2)}, u32[]{:S(2)}) %collective-permute-start.8) | collective-permute-done | bytes 696352 | tf_op jit(solution)/shard_map/ppermute | solution.py:190
  62.1 0.0 copy-done
  62.1 0.9 copy-done.2
  63.0 2.8 %merge.3 = (f32[32,2176]{1,0:T(8,128)}, f32[32,2176]{1,0:T(8,128)}, f32[32,2176]{1,0:T(8,128)}, f32[32,2176]{1,0:T(8,128)}) custom-call(f32[80,2176]{1,0:T(8,128)} %get-tuple-element.31.refs_0_, f32[80,2176]{1,0:T(8,128)} %copy-done, f32[80,2176]{1,0:T(8,128)} %copy-done.1, f32[80,2176]{1,0:T(8,128)} %copy-done.2), custom_call_target="tpu_custom_call" | custom-call | tf_op jit(solution)/shard_map/merge/pallas_call | solution.py:142
  65.8 7.4 %collective-permute-start.9 = (f32[32,2176]{1,0:T(8,128)}, f32[32,2176]{1,0:T(8,128)S(1)}, u32[]{:S(2)}, u32[]{:S(2)}) collective-permute-start(f32[32,2176]{1,0:T(8,128)} %get-tuple-element.36), channel_id=1, source_target_pairs={{0,64},{16,80},{32,96},{48,112},{64,0},{80,16},{96,32},{112,48},{1... | collective-permute-start | bytes 835592 | tf_op jit(solution)/shard_map/ppermute | solution.py:190
  73.2 2.0 %collective-permute-start.10 = (f32[32,2176]{1,0:T(8,128)}, f32[32,2176]{1,0:T(8,128)S(1)}, u32[]{:S(2)}, u32[]{:S(2)}) collective-permute-start(f32[32,2176]{1,0:T(8,128)} %get-tuple-element.37), channel_id=1, source_target_pairs={{0,128},{16,144},{32,160},{48,176},{64,192},{80,208},{96,224},{112... | collective-permute-start | bytes 835592 | tf_op jit(solution)/shard_map/ppermute | solution.py:190
  75.2 0.0 collective-permute-done.3.refs_2_
  75.2 0.4 collective-permute-start.11
  75.6 0.0 collective-permute-done.4.refs_3_
  75.6 0.0 collective-permute-done.5.refs_4_
  75.6 0.0 copy-start.7
  75.6 1.7 %collective-permute-done.9.refs_6_ = f32[32,2176]{1,0:T(8,128)S(1)} collective-permute-done((f32[32,2176]{1,0:T(8,128)}, f32[32,2176]{1,0:T(8,128)S(1)}, u32[]{:S(2)}, u32[]{:S(2)}) %collective-permute-start.9) | collective-permute-done | bytes 278560 | tf_op jit(solution)/shard_map/ppermute | solution.py:190
  77.3 6.0 %collective-permute-done.10.refs_7_ = f32[32,2176]{1,0:T(8,128)S(1)} collective-permute-done((f32[32,2176]{1,0:T(8,128)}, f32[32,2176]{1,0:T(8,128)S(1)}, u32[]{:S(2)}, u32[]{:S(2)}) %collective-permute-start.10) | collective-permute-done | bytes 278560 | tf_op jit(solution)/shard_map/ppermute | solution.py:190
  83.4 2.3 %collective-permute-done.11.refs_8_ = f32[32,2176]{1,0:T(8,128)S(1)} collective-permute-done((f32[32,2176]{1,0:T(8,128)}, f32[32,2176]{1,0:T(8,128)S(1)}, u32[]{:S(2)}, u32[]{:S(2)}) %collective-permute-start.11) | collective-permute-done | bytes 278560 | tf_op jit(solution)/shard_map/ppermute | solution.py:190
  85.7 0.0 copy-done.5
  85.7 0.7 copy-done.10
  86.4 4.0 %finish.1 = (f32[16,2,2048]{2,1,0:T(2,128)}, f32[16,2,128]{2,1,0:T(2,128)}) custom-call(s32[16]{0:T(128)} %refs_0_.1, f32[32,2176]{1,0:T(8,128)} %get-tuple-element.27.refs_1_, f32[32,2176]{1,0:T(8,128)} %copy-done.5, f32[32,2176]{1,0:T(8,128)} %copy-done.6, f32[32,2176]{1,0:T(8,128)} %copy-done.7, f32[32,2176]{1,0:T(8,128)} %get-tuple-element.35.refs_5_, ...), custom_call_target="tpu_custom_call" | custom-call | tf_op jit(solution)/shard_map/finish/pallas_call | solution.py:169
  90.4 5.9 %collective-permute-start.12 = (f32[16,2,128]{2,1,0:T(2,128)}, f32[16,2,128]{2,1,0:T(2,128)S(1)}, u32[]{:S(2)}, u32[]{:S(2)}) collective-permute-start(f32[16,2,128]{2,1,0:T(2,128)} %get-tuple-element.40), channel_id=1, source_target_pairs={{0,1},{1,0},{2,3},{3,2},{4,5},{5,4},{6,7},{7,6},{8,9},{9,8},{10,11... | collective-permute-start | bytes 49160 | tf_op jit(solution)/shard_map/ppermute | solution.py:190
  96.4 1.0 collective-permute-done.12
  97.4 0.7 add.12
  98.1 1.7 %collective-permute-start.13 = (f32[16,2,128]{2,1,0:T(2,128)S(1)}, f32[16,2,128]{2,1,0:T(2,128)S(1)}, u32[]{:S(2)}, u32[]{:S(2)}) collective-permute-start(f32[16,2,128]{2,1,0:T(2,128)S(1)} %add.12), channel_id=1, source_target_pairs={{0,2},{1,3},{2,0},{3,1},{4,6},{5,7},{6,4},{7,5},{8,10},{9,11},{10,... | collective-permute-start | bytes 49160 | tf_op jit(solution)/shard_map/ppermute | solution.py:190
  99.9 1.1 collective-permute-done.13
  101.0 4.3 %collective-permute-start.14 = (f32[16,2,128]{2,1,0:T(2,128)S(1)}, f32[16,2,128]{2,1,0:T(2,128)S(1)}, u32[]{:S(2)}, u32[]{:S(2)}) collective-permute-start(f32[16,2,128]{2,1,0:T(2,128)S(1)} %add.13), channel_id=1, source_target_pairs={{0,6},{1,7},{2,4},{3,5},{4,2},{5,3},{6,0},{7,1},{8,14},{9,15},{10,... | collective-permute-start | bytes 49160 | tf_op jit(solution)/shard_map/ppermute | solution.py:190
  105.3 1.1 collective-permute-done.14
  106.4 4.6 %collective-permute-start.15 = (f32[16,2,128]{2,1,0:T(2,128)S(1)}, f32[16,2,128]{2,1,0:T(2,128)S(1)}, u32[]{:S(2)}, u32[]{:S(2)}) collective-permute-start(f32[16,2,128]{2,1,0:T(2,128)S(1)} %add.14), channel_id=1, source_target_pairs={{0,14},{1,15},{2,12},{3,13},{4,10},{5,11},{6,8},{7,9},{8,6},{9,7},... | collective-permute-start | bytes 49160 | tf_op jit(solution)/shard_map/ppermute | solution.py:190
  111.0 1.1 collective-permute-done.15
  112.1 0.1 copy.8
  112.2 0.1 copy.9
  112.3 1.8 %subtract_bitcast_fusion = f32[1,16,2,2048]{3,2,1,0:T(2,128)} fusion(f32[16,2,2048]{2,1,0:T(2,128)} %get-tuple-element.39, f32[16,2]{1,0:T(8,128)S(1)} %copy.9), kind=kLoop, calls=%fused_computation | loop fusion | flops 65536 | bytes 524416 | tf_op jit(solution)/shard_map/broadcast_in_dim | solution.py:209
  (17 shorter events, 0.1 us)
Async XLA Ops:
  12.3 16.4 %collective-permute-start = (f32[80,2176]{1,0:T(8,128)}, f32[80,2176]{1,0:T(8,128)S(1)}, u32[]{:S(2)}, u32[]{:S(2)}) collective-permute-start(f32[80,2176]{1,0:T(8,128)} %get-tuple-element.24), channel_id=1, source_target_pairs={{0,64},{16,80},{32,96},{48,112},{64,0},{80,16},{96,32},{112,48},{1... | collective-permute-start | bytes 2088968 | tf_op jit(solution)/shard_map/ppermute | solution.py:190
  14.3 32.7 %collective-permute-start.1 = (f32[80,2176]{1,0:T(8,128)}, f32[80,2176]{1,0:T(8,128)S(1)}, u32[]{:S(2)}, u32[]{:S(2)}) collective-permute-start(f32[80,2176]{1,0:T(8,128)} %get-tuple-element.25), channel_id=1, source_target_pairs={{0,128},{16,144},{32,160},{48,176},{64,192},{80,208},{96,224},{112... | collective-permute-start | bytes 2088968 | tf_op jit(solution)/shard_map/ppermute | solution.py:190
  16.7 32.4 %collective-permute-start.2 = (f32[80,2176]{1,0:T(8,128)}, f32[80,2176]{1,0:T(8,128)}, u32[]{:S(2)}, u32[]{:S(2)}) collective-permute-start(f32[80,2176]{1,0:T(8,128)} %get-tuple-element.26), channel_id=1, source_target_pairs={{0,192},{16,208},{32,224},{48,240},{64,128},{80,144},{96,160},{112... | collective-permute-start | bytes 2088968 | tf_op jit(solution)/shard_map/ppermute | solution.py:190
  16.7 39.1 %collective-permute-start.6 = (f32[80,2176]{1,0:T(8,128)}, f32[80,2176]{1,0:T(8,128)S(1)}, u32[]{:S(2)}, u32[]{:S(2)}) collective-permute-start(f32[80,2176]{1,0:T(8,128)} %get-tuple-element.32), channel_id=1, source_target_pairs={{0,16},{16,0},{32,48},{48,32},{64,80},{80,64},{96,112},{112,96},{1... | collective-permute-start | bytes 2088968 | tf_op jit(solution)/shard_map/ppermute | solution.py:190
  18.2 37.6 %collective-permute-start.7 = (f32[80,2176]{1,0:T(8,128)}, f32[80,2176]{1,0:T(8,128)S(1)}, u32[]{:S(2)}, u32[]{:S(2)}) collective-permute-start(f32[80,2176]{1,0:T(8,128)} %get-tuple-element.33), channel_id=1, source_target_pairs={{0,32},{16,48},{32,0},{48,16},{64,96},{80,112},{96,64},{112,80},{1... | collective-permute-start | bytes 2088968 | tf_op jit(solution)/shard_map/ppermute | solution.py:190
  28.7 20.5 %copy-start.3 = (f32[80,2176]{1,0:T(8,128)}, f32[80,2176]{1,0:T(8,128)S(1)}, u32[]{:S(2)}) copy-start(f32[80,2176]{1,0:T(8,128)S(1)} %collective-permute-done.refs_1_) | copy-start | bytes 2088964
  28.7 33.4 %collective-permute-start.8 = (f32[80,2176]{1,0:T(8,128)}, f32[80,2176]{1,0:T(8,128)S(1)}, u32[]{:S(2)}, u32[]{:S(2)}) collective-permute-start(f32[80,2176]{1,0:T(8,128)} %get-tuple-element.34), channel_id=1, source_target_pairs={{0,48},{16,32},{32,16},{48,0},{64,112},{80,96},{96,80},{112,64},{1... | collective-permute-start | bytes 2088968 | tf_op jit(solution)/shard_map/ppermute | solution.py:190
  46.9 2.2 %copy-start.4 = (f32[80,2176]{1,0:T(8,128)}, f32[80,2176]{1,0:T(8,128)S(1)}, u32[]{:S(2)}) copy-start(f32[80,2176]{1,0:T(8,128)S(1)} %collective-permute-done.1.refs_2_) | copy-start | bytes 2088964
  51.9 23.3 %collective-permute-start.3 = (f32[32,2176]{1,0:T(8,128)}, f32[32,2176]{1,0:T(8,128)S(1)}, u32[]{:S(2)}, u32[]{:S(2)}) collective-permute-start(f32[32,2176]{1,0:T(8,128)} %get-tuple-element.28), channel_id=1, source_target_pairs={{0,16},{16,0},{32,48},{48,32},{64,80},{80,64},{96,112},{112,96},{1... | collective-permute-start | bytes 835592 | tf_op jit(solution)/shard_map/ppermute | solution.py:190
  53.2 22.4 %collective-permute-start.4 = (f32[32,2176]{1,0:T(8,128)}, f32[32,2176]{1,0:T(8,128)S(1)}, u32[]{:S(2)}, u32[]{:S(2)}) collective-permute-start(f32[32,2176]{1,0:T(8,128)} %get-tuple-element.29), channel_id=1, source_target_pairs={{0,32},{16,48},{32,0},{48,16},{64,96},{80,112},{96,64},{112,80},{1... | collective-permute-start | bytes 835592 | tf_op jit(solution)/shard_map/ppermute | solution.py:190
  55.8 6.3 %copy-start = (f32[80,2176]{1,0:T(8,128)}, f32[80,2176]{1,0:T(8,128)S(1)}, u32[]{:S(2)}) copy-start(f32[80,2176]{1,0:T(8,128)S(1)} %collective-permute-done.6.refs_1_) | copy-start | bytes 2088964
  55.8 19.7 %collective-permute-start.5 = (f32[32,2176]{1,0:T(8,128)}, f32[32,2176]{1,0:T(8,128)S(1)}, u32[]{:S(2)}, u32[]{:S(2)}) collective-permute-start(f32[32,2176]{1,0:T(8,128)} %get-tuple-element.30), channel_id=1, source_target_pairs={{0,48},{16,32},{32,16},{48,0},{64,112},{80,96},{96,80},{112,64},{1... | collective-permute-start | bytes 835592 | tf_op jit(solution)/shard_map/ppermute | solution.py:190
  55.9 6.3 %copy-start.1 = (f32[80,2176]{1,0:T(8,128)}, f32[80,2176]{1,0:T(8,128)S(1)}, u32[]{:S(2)}) copy-start(f32[80,2176]{1,0:T(8,128)S(1)} %collective-permute-done.7.refs_2_) | copy-start | bytes 2088964
  62.1 0.9 copy-start.2
  65.8 11.5 %collective-permute-start.9 = (f32[32,2176]{1,0:T(8,128)}, f32[32,2176]{1,0:T(8,128)S(1)}, u32[]{:S(2)}, u32[]{:S(2)}) collective-permute-start(f32[32,2176]{1,0:T(8,128)} %get-tuple-element.36), channel_id=1, source_target_pairs={{0,64},{16,80},{32,96},{48,112},{64,0},{80,16},{96,32},{112,48},{1... | collective-permute-start | bytes 835592 | tf_op jit(solution)/shard_map/ppermute | solution.py:190
  73.2 10.2 %collective-permute-start.10 = (f32[32,2176]{1,0:T(8,128)}, f32[32,2176]{1,0:T(8,128)S(1)}, u32[]{:S(2)}, u32[]{:S(2)}) collective-permute-start(f32[32,2176]{1,0:T(8,128)} %get-tuple-element.37), channel_id=1, source_target_pairs={{0,128},{16,144},{32,160},{48,176},{64,192},{80,208},{96,224},{112... | collective-permute-start | bytes 835592 | tf_op jit(solution)/shard_map/ppermute | solution.py:190
  75.2 10.5 %copy-start.5 = (f32[32,2176]{1,0:T(8,128)}, f32[32,2176]{1,0:T(8,128)S(1)}, u32[]{:S(2)}) copy-start(f32[32,2176]{1,0:T(8,128)S(1)} %collective-permute-done.3.refs_2_) | copy-start | bytes 835588
  75.2 10.5 %collective-permute-start.11 = (f32[32,2176]{1,0:T(8,128)}, f32[32,2176]{1,0:T(8,128)S(1)}, u32[]{:S(2)}, u32[]{:S(2)}) collective-permute-start(f32[32,2176]{1,0:T(8,128)} %get-tuple-element.38), channel_id=1, source_target_pairs={{0,192},{16,208},{32,224},{48,240},{64,128},{80,144},{96,160},{112... | collective-permute-start | bytes 835592 | tf_op jit(solution)/shard_map/ppermute | solution.py:190
  75.6 10.1 %copy-start.6 = (f32[32,2176]{1,0:T(8,128)}, f32[32,2176]{1,0:T(8,128)S(1)}, u32[]{:S(2)}) copy-start(f32[32,2176]{1,0:T(8,128)S(1)} %collective-permute-done.4.refs_3_) | copy-start | bytes 835588
  75.6 10.1 %copy-start.7 = (f32[32,2176]{1,0:T(8,128)}, f32[32,2176]{1,0:T(8,128)S(1)}, u32[]{:S(2)}) copy-start(f32[32,2176]{1,0:T(8,128)S(1)} %collective-permute-done.5.refs_4_) | copy-start | bytes 835588
  77.3 8.4 %copy-start.8 = (f32[32,2176]{1,0:T(8,128)}, f32[32,2176]{1,0:T(8,128)S(1)}, u32[]{:S(2)}) copy-start(f32[32,2176]{1,0:T(8,128)S(1)} %collective-permute-done.9.refs_6_) | copy-start | bytes 835588
  83.4 2.4 %copy-start.9 = (f32[32,2176]{1,0:T(8,128)}, f32[32,2176]{1,0:T(8,128)S(1)}, u32[]{:S(2)}) copy-start(f32[32,2176]{1,0:T(8,128)S(1)} %collective-permute-done.10.refs_7_) | copy-start | bytes 835588
  85.7 0.7 copy-start.10
  90.4 7.0 %collective-permute-start.12 = (f32[16,2,128]{2,1,0:T(2,128)}, f32[16,2,128]{2,1,0:T(2,128)S(1)}, u32[]{:S(2)}, u32[]{:S(2)}) collective-permute-start(f32[16,2,128]{2,1,0:T(2,128)} %get-tuple-element.40), channel_id=1, source_target_pairs={{0,1},{1,0},{2,3},{3,2},{4,5},{5,4},{6,7},{7,6},{8,9},{9,8},{10,11... | collective-permute-start | bytes 49160 | tf_op jit(solution)/shard_map/ppermute | solution.py:190
  98.1 2.9 %collective-permute-start.13 = (f32[16,2,128]{2,1,0:T(2,128)S(1)}, f32[16,2,128]{2,1,0:T(2,128)S(1)}, u32[]{:S(2)}, u32[]{:S(2)}) collective-permute-start(f32[16,2,128]{2,1,0:T(2,128)S(1)} %add.12), channel_id=1, source_target_pairs={{0,2},{1,3},{2,0},{3,1},{4,6},{5,7},{6,4},{7,5},{8,10},{9,11},{10,... | collective-permute-start | bytes 49160 | tf_op jit(solution)/shard_map/ppermute | solution.py:190
  101.0 5.4 %collective-permute-start.14 = (f32[16,2,128]{2,1,0:T(2,128)S(1)}, f32[16,2,128]{2,1,0:T(2,128)S(1)}, u32[]{:S(2)}, u32[]{:S(2)}) collective-permute-start(f32[16,2,128]{2,1,0:T(2,128)S(1)} %add.13), channel_id=1, source_target_pairs={{0,6},{1,7},{2,4},{3,5},{4,2},{5,3},{6,0},{7,1},{8,14},{9,15},{10,... | collective-permute-start | bytes 49160 | tf_op jit(solution)/shard_map/ppermute | solution.py:190
  106.4 5.7 %collective-permute-start.15 = (f32[16,2,128]{2,1,0:T(2,128)S(1)}, f32[16,2,128]{2,1,0:T(2,128)S(1)}, u32[]{:S(2)}, u32[]{:S(2)}) collective-permute-start(f32[16,2,128]{2,1,0:T(2,128)S(1)} %add.14), channel_id=1, source_target_pairs={{0,14},{1,15},{2,12},{3,13},{4,10},{5,11},{6,8},{7,9},{8,6},{9,7},... | collective-permute-start | bytes 49160 | tf_op jit(solution)/shard_map/ppermute | solution.py:190
